TPU v7x, 512 devices: a whole 4x8x8 slice. The times are simulated.
512 devices in a mesh: energy: 128 (over z, y, core), transpor: 4 (over x).
Axes of the slice: x: 4, y: 8, z: 8, core: 2. Of those that a mesh axis runs over, the one named last changes fastest.
Arguments:
- onsite: float32 [4, 128, 128], P('transpor'), may hold values from -1 to 1, as said below
- hopping: float32 [4, 128, 128], P('transpor'), may hold values from -0.25 to 0.25
- selfenergy: float32 [128, 4, 128, 128], P('energy', 'transpor'), may hold values from -1 to 1, as said below
- broadening: float32 [128, 4, 128], P('energy', 'transpor'), may hold values from 0.1 to 0.5
Outputs:
- green: float32 [128, 2, 4, 128, 128], P('energy', None, 'transpor')
- polar: float32 [128, 2, 4, 128, 128], P('energy', None, 'transpor')
Inputs may be any that keep to these rules, and one draw needn't show every extreme that they name: `onsite`: each block is symmetric. `selfenergy`: each block is symmetric.
All inputs are finite; a program needn't handle non-finite values.
Results may differ from a plain program's by a relative error of at most 0.00021.
Values sent between devices are 32-bit elements; how exact they have to be, the bound alone decides.
A program may use at most 128 MiB of HBM per device.

v0:
```python
import math
import jax
import jax.numpy as jnp
from jax import lax
from jax.sharding import PartitionSpec as P

ENERGY_LOW = -1.5
ENERGY_HIGH = 1.5


def prefix_2(part, axis, combine, identity, reverse):
    count = lax.axis_size(axis)
    place = lax.axis_index(axis)
    ahead = count - 1 - place if reverse else place
    gathered = jax.tree.map(lambda a: lax.all_gather(a, axis), part)
    state = jax.tree.map(lambda a, e: jnp.zeros_like(a) + jnp.asarray(e, a.dtype), part, identity)

    def one(hop, state):
        source = count - 1 - hop if reverse else hop
        return combine(
            state, jax.tree.map(lambda a: lax.dynamic_index_in_dim(a, source, 0, False), gathered)
        )

    return lax.fori_loop(0, ahead, one, state)


def product(left, right):
    return jnp.matmul(left, right, precision=lax.Precision.HIGHEST)


def flipped(matrix):
    return jnp.swapaxes(matrix, -1, -2)


def complex_mul(first, second):
    return (
        product(first[0], second[0]) - product(first[1], second[1]),
        product(first[0], second[1]) + product(first[1], second[0]),
    )


def complex_add(first, second):
    return (first[0] + second[0], first[1] + second[1])


def complex_flip(value):
    return (flipped(value[0]), flipped(value[1]))


def real_left(matrix, value):
    return (product(matrix, value[0]), product(matrix, value[1]))


def real_right(value, matrix):
    return (product(value[0], matrix), product(value[1], matrix))


def invert(value):
    real_part, imag_part = value
    normal_real = product(flipped(real_part), real_part) + product(flipped(imag_part), imag_part)
    normal_imag = product(flipped(real_part), imag_part) - product(flipped(imag_part), real_part)
    upper_rows = jnp.concatenate([normal_real, -normal_imag], -1)
    lower_rows = jnp.concatenate([normal_imag, normal_real], -1)
    factor = jnp.linalg.cholesky(jnp.concatenate([upper_rows, lower_rows], -2))
    target = jnp.concatenate([flipped(real_part), -flipped(imag_part)], -2)
    solved = jax.scipy.linalg.cho_solve((factor, True), target)
    orders = real_part.shape[-1]
    return (solved[..., :orders, :], solved[..., orders:, :])


def joined(left, right, coupling):
    first_a, cross_a, last_a = left
    first_b, cross_b, last_b = right
    unit_matrix = jnp.eye(coupling.shape[-1], dtype=jnp.float32)
    dressing = real_right(real_left(coupling, first_b), flipped(coupling))
    loaded = complex_mul(last_a, dressing)
    kernel = invert((unit_matrix - loaded[0], -loaded[1]))
    weighted = complex_mul(kernel, last_a)
    first_new = complex_add(
        first_a,
        complex_mul(complex_mul(cross_a, complex_mul(dressing, kernel)), complex_flip(cross_a)),
    )
    bridge = real_left(coupling, cross_b)
    lifted = complex_add(cross_a, complex_mul(cross_a, complex_mul(dressing, weighted)))
    cross_new = complex_mul(lifted, bridge)
    last_new = complex_add(last_b, complex_mul(complex_flip(bridge), complex_mul(weighted, bridge)))
    return (first_new, cross_new, last_new)


def packed(corners, coupling, marker):
    return (
        corners[0][0],
        corners[0][1],
        corners[1][0],
        corners[1][1],
        corners[2][0],
        corners[2][1],
        coupling,
        marker,
    )


def unpacked(element):
    return ((element[0], element[1]), (element[2], element[3]), (element[4], element[5]))


def tree_join(earlier, later):
    merged = packed(
        joined(unpacked(earlier), unpacked(later), earlier[6]),
        later[6],
        jnp.maximum(earlier[7], later[7]),
    )
    has_early = earlier[7][0] > 0
    has_late = later[7][0] > 0
    return tuple(
        (
            jnp.where(has_early, jnp.where(has_late, whole_part, early_part), late_part)
            for whole_part, early_part, late_part in zip(merged, earlier, later)
        )
    )


def reverse_join(earlier, later):
    return tree_join(later, earlier)


def transform_sum(values):
    energy_total = values.shape[0]
    length = 2 * energy_total
    phase = (
        jnp.arange(length, dtype=jnp.int32)[:, None]
        * jnp.arange(energy_total, dtype=jnp.int32)[None, :]
        % length
    )
    angles = phase.astype(jnp.float32) * (2.0 * math.pi / length)
    cosine = jnp.cos(angles)
    sine_table = jnp.sin(angles)
    trailing = values.shape[2:]
    real_flat = values[:, 0].reshape(energy_total, -1)
    imag_flat = values[:, 1].reshape(energy_total, -1)
    spec_real = product(cosine, real_flat) + product(sine_table, imag_flat)
    spec_imag = product(cosine, imag_flat) - product(sine_table, real_flat)
    power = spec_real * spec_real + spec_imag * spec_imag
    real_sum = product(flipped(cosine), power) / (length * energy_total)
    imag_sum = product(flipped(sine_table), power) / (length * energy_total)
    return jnp.stack(
        [
            real_sum.reshape((energy_total,) + trailing),
            imag_sum.reshape((energy_total,) + trailing),
        ],
        1,
    )


def on_device(onsite, hopping, selfenergy, broadening):
    per_energy = selfenergy.shape[0]
    blocks = onsite.shape[0]
    orders = onsite.shape[-1]
    axis_span = lax.axis_size("transpor")
    energy_count = per_energy * lax.axis_size("energy")
    first_energy = lax.axis_index("energy") * per_energy
    levels = (
        ENERGY_LOW
        + (ENERGY_HIGH - ENERGY_LOW)
        * ((first_energy + jnp.arange(per_energy, dtype=jnp.int32)).astype(jnp.float32) + 0.5)
        / energy_count
    )
    unit_matrix = jnp.eye(orders, dtype=jnp.float32)
    outgoing = hopping[blocks - 1]
    at_end = (lax.axis_index("transpor") == axis_span - 1).astype(jnp.float32)
    contact = at_end * product(outgoing, flipped(outgoing))
    block_index = 0
    real_part = (
        levels[:, None, None] * unit_matrix - onsite[block_index] - selfenergy[:, block_index]
    )
    imag_part = broadening[:, block_index, :, None] * unit_matrix
    imag_part = imag_part + contact
    matrices = [(real_part, imag_part)]
    singles = [invert(matrix) for matrix in matrices]
    segment = (singles[0], singles[0], singles[0])
    element = packed(segment, outgoing, jnp.ones((1,), jnp.float32))
    neutral = tuple((jnp.zeros_like(member) for member in element))
    prefix = prefix_2(element, "transpor", tree_join, neutral, False)
    suffix = prefix_2(element, "transpor", reverse_join, neutral, True)
    sigma_left = real_right(real_left(flipped(prefix[6]), (prefix[4], prefix[5])), prefix[6])
    sigma_right = real_right(real_left(outgoing, (suffix[0], suffix[1])), flipped(outgoing))
    block_index = 0
    real_part, imag_part = matrices[block_index]
    real_part = real_part - sigma_left[0]
    imag_part = imag_part - sigma_left[1]
    real_part = real_part - sigma_right[0]
    imag_part = imag_part - sigma_right[1]
    connected = [invert((real_part, imag_part))]
    greens = [connected[-1]]
    green = jnp.stack(
        [
            jnp.stack([value_pair[0] for value_pair in greens], 1),
            jnp.stack([value_pair[1] for value_pair in greens], 1),
        ],
        1,
    )
    flattened = green.reshape(per_energy, 2, blocks, orders * orders)
    correlated = transform_sum(
        lax.all_to_all(flattened, "energy", split_axis=3, concat_axis=0, tiled=True)
    )
    returned = lax.all_to_all(correlated, "energy", split_axis=0, concat_axis=3, tiled=True)
    polar = returned.reshape(per_energy, 2, blocks, orders, orders)
    return (green, polar)


def solution(mesh):
    placed = (
        P("transpor", None, None),
        P("transpor", None, None),
        P("energy", "transpor", None, None),
        P("energy", "transpor", None),
    )
    return jax.shard_map(
        on_device,
        mesh=mesh,
        in_specs=placed,
        out_specs=(
            P("energy", None, "transpor", None, None),
            P("energy", None, "transpor", None, None),
        ),
        check_vma=False,
    )
```

profile of v0, /device:TPU:1, one launch (start us, length us, event | category | flops | bytes accessed | tf_op | source)
XLA Modules:
  0.0 622.7 jit_solution(16338300515268233573)
XLA Ops:
  5.0 11.7 %custom-call.41 = f32[1,128,128]{2,1,0:T(8,128)S(1)} custom-call(f32[1,128,128]{2,1,0:T(8,128)S(1)} %slice.245), custom_call_target="Cholesky" | custom-call | tf_op jit(solution)/shard_map/jit(cholesky)/cholesky/custom-call.2 | solution.py:64
  16.8 9.8 %custom-call.42 = f32[1,1,128,128]{2,3,1,0:T(8,128)S(1)} custom-call(f32[1,1,128,128]{3,2,1,0:T(8,128)S(1)} %get-tuple-element.618), custom_call_target="InvertDiagBlocksLowerTriangular" | custom-call | tf_op jit(solution)/shard_map/jit(cholesky)/cholesky/custom-call.5 | solution.py:64
  27.3 10.7 %all_gather.17 = f32[4,128,128]{2,1,0:T(8,128)S(1)} all-gather(f32[1,128,128]{2,1,0:T(8,128)} %param.14), channel_id=1, replica_groups=mesh['energy'=128,'transpor'=4] {'transpor'}, dimensions={0}, use_global_device_ids=true | all-gather | bytes 327680 | tf_op jit(solution)/shard_map/all_gather | solution.py:15
  40.0 8.3 %all-reduce.1 = f32[4]{0:T(128)S(1)} all-reduce(f32[4]{0:T(128)S(1)} %dynamic-update-slice.23), channel_id=1, replica_groups=mesh['energy'=128,'transpor'=4] {'transpor'}, use_global_device_ids=true, to_apply=%add.1 | all-reduce | flops 4 | bytes 32
  48.2 11.7 %custom-call.43 = f32[1,128,128]{2,1,0:T(8,128)S(1)} custom-call(f32[1,128,128]{2,1,0:T(8,128)S(1)} %fusion.147), custom_call_target="Cholesky" | custom-call | tf_op jit(solution)/shard_map/jit(cholesky)/cholesky/custom-call.3 | solution.py:64
  62.1 3.9 while.67
  62.7 1.3 bitcast_dynamic-update-slice_fusion.16
  64.7 1.3 bitcast_dynamic-update-slice_fusion.16
  66.1 19.7 %custom-call.45 = f32[2,128,128]{1,2,0:T(8,128)S(1)} custom-call(f32[2,128,128]{2,1,0:T(8,128)S(1)} %get-tuple-element.401), custom_call_target="InvertDiagBlocksLowerTriangular" | custom-call | tf_op jit(solution)/shard_map/jit(_cho_solve)/triangular_solve/custom-call.4 | solution.py:66
  87.3 9.4 %all-gather = f32[4,128,128]{2,1,0:T(8,128)S(1)} all-gather(f32[1,128,128]{2,1,0:T(8,128)S(1)} %get-tuple-element.610), channel_id=2, replica_groups=mesh['energy'=128,'transpor'=4] {'transpor'}, dimensions={0}, use_global_device_ids=true | all-gather | bytes 327680 | tf_op jit(solution)/shard_map/all_gather | solution.py:15
  96.7 9.8 %all-gather.1 = f32[4,128,128]{2,1,0:T(8,128)S(1)} all-gather(f32[1,128,128]{2,1,0:T(8,128)S(1)} %get-tuple-element.609), channel_id=3, replica_groups=mesh['energy'=128,'transpor'=4] {'transpor'}, dimensions={0}, use_global_device_ids=true | all-gather | bytes 327680 | tf_op jit(solution)/shard_map/all_gather | solution.py:15
  106.5 12.2 %while.64 = (s32[]{:T(128)}, f32[1,128,128]{2,1,0:T(8,128)S(1)}, f32[1,128,128]{2,1,0:T(8,128)S(1)}, f32[128,128]{1,0:T(8,128)S(1)}, f32[1]{0:T(128)}, /*index=5...) while((s32[]{:T(128)}, f32[1,128,128]{2,1,0:T(8,128)S(1)}, ...), condition=%wide.region_5.9_spmd, body=%wide.region_4.8_spmd.sunk | while | flops 806813952 | bytes 11471332 | solution.py:24
  119.3 214.8 %while.66 = (s32[]{:T(128)}, f32[1,128,128]{2,1,0:T(8,128)S(1)}, f32[1,128,128]{2,1,0:T(8,128)S(1)}, f32[1]{0:T(128)}, s32[]{:T(128)}, /*index=5*/f32[4,1]{0,1:T...) while((s32[]{:T(128)}, f32[1,128,128]{2,1,0:T(8,128)S(1)}, ...), condition=%wide.region_7.11_spmd, body=%wide.region_6.10_spmd.sunk | while | flops 806764800 | bytes 11342354 | solution.py:24
  122.9 11.7 %custom-call.68 = f32[1,128,128]{2,1,0:T(8,128)S(1)} custom-call(f32[1,128,128]{2,1,0:T(8,128)S(1)} %slice.430), custom_call_target="Cholesky" | custom-call | tf_op jit(solution)/shard_map/while/body/jit(cholesky)/cholesky/custom-call.2 | solution.py:64
  134.6 9.8 %custom-call.69 = f32[1,1,128,128]{2,3,1,0:T(8,128)S(1)} custom-call(f32[1,1,128,128]{3,2,1,0:T(8,128)S(1)} %get-tuple-element.883), custom_call_target="InvertDiagBlocksLowerTriangular" | custom-call | tf_op jit(solution)/shard_map/while/body/jit(cholesky)/cholesky/custom-call.5 | solution.py:64
  145.0 11.7 %custom-call.70 = f32[1,128,128]{2,1,0:T(8,128)S(1)} custom-call(f32[1,128,128]{2,1,0:T(8,128)S(1)} %fusion.661), custom_call_target="Cholesky" | custom-call | tf_op jit(solution)/shard_map/while/body/jit(cholesky)/cholesky/custom-call.3 | solution.py:64
  159.0 4.0 while.70
  159.6 1.3 bitcast_dynamic-update-slice_fusion.18
  161.6 1.3 bitcast_dynamic-update-slice_fusion.18
  163.0 19.7 %custom-call.72 = f32[2,128,128]{1,2,0:T(8,128)S(1)} custom-call(f32[2,128,128]{2,1,0:T(8,128)S(1)} %get-tuple-element.889), custom_call_target="InvertDiagBlocksLowerTriangular" | custom-call | tf_op jit(solution)/shard_map/while/body/jit(_cho_solve)/triangular_solve/custom-call.4 | solution.py:66
  194.3 11.7 %custom-call.68 = f32[1,128,128]{2,1,0:T(8,128)S(1)} custom-call(f32[1,128,128]{2,1,0:T(8,128)S(1)} %slice.430), custom_call_target="Cholesky" | custom-call | tf_op jit(solution)/shard_map/while/body/jit(cholesky)/cholesky/custom-call.2 | solution.py:64
  206.1 9.8 %custom-call.69 = f32[1,1,128,128]{2,3,1,0:T(8,128)S(1)} custom-call(f32[1,1,128,128]{3,2,1,0:T(8,128)S(1)} %get-tuple-element.883), custom_call_target="InvertDiagBlocksLowerTriangular" | custom-call | tf_op jit(solution)/shard_map/while/body/jit(cholesky)/cholesky/custom-call.5 | solution.py:64
  216.5 11.7 %custom-call.70 = f32[1,128,128]{2,1,0:T(8,128)S(1)} custom-call(f32[1,128,128]{2,1,0:T(8,128)S(1)} %fusion.661), custom_call_target="Cholesky" | custom-call | tf_op jit(solution)/shard_map/while/body/jit(cholesky)/cholesky/custom-call.3 | solution.py:64
  230.4 4.0 while.70
  231.1 1.3 bitcast_dynamic-update-slice_fusion.18
  234.4 19.7 %custom-call.72 = f32[2,128,128]{1,2,0:T(8,128)S(1)} custom-call(f32[2,128,128]{2,1,0:T(8,128)S(1)} %get-tuple-element.889), custom_call_target="InvertDiagBlocksLowerTriangular" | custom-call | tf_op jit(solution)/shard_map/while/body/jit(_cho_solve)/triangular_solve/custom-call.4 | solution.py:66
  265.8 11.7 %custom-call.68 = f32[1,128,128]{2,1,0:T(8,128)S(1)} custom-call(f32[1,128,128]{2,1,0:T(8,128)S(1)} %slice.430), custom_call_target="Cholesky" | custom-call | tf_op jit(solution)/shard_map/while/body/jit(cholesky)/cholesky/custom-call.2 | solution.py:64
  277.5 9.8 %custom-call.69 = f32[1,1,128,128]{2,3,1,0:T(8,128)S(1)} custom-call(f32[1,1,128,128]{3,2,1,0:T(8,128)S(1)} %get-tuple-element.883), custom_call_target="InvertDiagBlocksLowerTriangular" | custom-call | tf_op jit(solution)/shard_map/while/body/jit(cholesky)/cholesky/custom-call.5 | solution.py:64
  287.9 11.7 %custom-call.70 = f32[1,128,128]{2,1,0:T(8,128)S(1)} custom-call(f32[1,128,128]{2,1,0:T(8,128)S(1)} %fusion.661), custom_call_target="Cholesky" | custom-call | tf_op jit(solution)/shard_map/while/body/jit(cholesky)/cholesky/custom-call.3 | solution.py:64
  301.9 4.0 while.70
  305.9 19.7 %custom-call.72 = f32[2,128,128]{1,2,0:T(8,128)S(1)} custom-call(f32[2,128,128]{2,1,0:T(8,128)S(1)} %get-tuple-element.889), custom_call_target="InvertDiagBlocksLowerTriangular" | custom-call | tf_op jit(solution)/shard_map/while/body/jit(_cho_solve)/triangular_solve/custom-call.4 | solution.py:66
  337.0 11.7 %custom-call.46 = f32[1,128,128]{2,1,0:T(8,128)S(1)} custom-call(f32[1,128,128]{2,1,0:T(8,128)S(1)} %slice.255), custom_call_target="Cholesky" | custom-call | tf_op jit(solution)/shard_map/jit(cholesky)/cholesky/custom-call.2 | solution.py:64
  348.8 9.8 %custom-call.47 = f32[1,1,128,128]{2,3,1,0:T(8,128)S(1)} custom-call(f32[1,1,128,128]{3,2,1,0:T(8,128)S(1)} %get-tuple-element.614), custom_call_target="InvertDiagBlocksLowerTriangular" | custom-call | tf_op jit(solution)/shard_map/jit(cholesky)/cholesky/custom-call.5 | solution.py:64
  359.3 11.7 %custom-call.48 = f32[1,128,128]{2,1,0:T(8,128)S(1)} custom-call(f32[1,128,128]{2,1,0:T(8,128)S(1)} %fusion.150), custom_call_target="Cholesky" | custom-call | tf_op jit(solution)/shard_map/jit(cholesky)/cholesky/custom-call.3 | solution.py:64
  373.8 4.3 while.68
  374.6 1.4 bitcast_dynamic-update-slice_fusion.17
  376.7 1.4 bitcast_dynamic-update-slice_fusion.17
  378.1 19.7 %custom-call.50 = f32[2,128,128]{1,2,0:T(8,128)S(1)} custom-call(f32[2,128,128]{2,1,0:T(8,128)S(1)} %get-tuple-element.403), custom_call_target="InvertDiagBlocksLowerTriangular" | custom-call | tf_op jit(solution)/shard_map/jit(_cho_solve)/triangular_solve/custom-call.4 | solution.py:66
  399.4 12.1 %copy.118 = f32[1,1,1,16384]{1,2,0,3:T(1,128)} copy(f32[1,1,1,16384]{3,2,1,0:T(1,128)S(1)} %bitcast.935) | data formatting | bytes 131072 | tf_op jit(solution)/shard_map/stack | solution.py:195
  411.4 11.9 %copy.117 = f32[1,1,1,16384]{1,2,0,3:T(1,128)} copy(f32[1,1,1,16384]{3,2,1,0:T(1,128)S(1)} %bitcast.934) | data formatting | bytes 131072 | tf_op jit(solution)/shard_map/stack | solution.py:195
  423.4 20.7 %fusion.252 = f32[16384,1,1,2]{3,2,1,0:T(1,128)} fusion(f32[1,1,1,16384]{1,2,0,3:T(1,128)} %copy.118, f32[1,1,1,16384]{1,2,0,3:T(1,128)} %copy.117), kind=kLoop, calls=%fused_computation.405 | loop fusion | flops 32768 | bytes 262144
  444.6 74.5 %reduce.94 = f32[16384,2]{1,0:T(8,128)} reduce(f32[16384,1,1,2]{3,2,1,0:T(1,128)} %fusion.252, f32[]{:T(128)} %broadcast.260), dimensions={1,2}, to_apply=%fusion.252.reduce_sub_computation | reduce | bytes 262148
  519.0 7.6 %reshape.504 = f32[128,1,256]{2,1,0:T(1,128)S(1)} reshape(f32[16384,2]{1,0:T(8,128)} %reduce.94) | data formatting | bytes 262144
  526.6 40.4 %all_to_all.33 = f32[128,1,256]{2,1,0:T(1,128)S(1)} all-to-all(f32[128,1,256]{2,1,0:T(1,128)S(1)} %reshape.504), channel_id=1, replica_groups=mesh['energy'=128,'transpor'=4] {'energy'}, dimensions={0} | all-to-all | bytes 262144 | tf_op jit(solution)/shard_map/all_to_all | solution.py:204
  568.0 14.9 %reshape.505 = f32[16384,1,1,2]{3,2,1,0:T(1,128)} reshape(f32[128,256]{1,0:T(8,128)S(1)} %reduce.95) | data formatting | bytes 262144
  582.9 15.0 %copy.119 = f32[1,2,1,16384]{3,2,1,0:T(1,128)S(1)} copy(f32[1,2,1,16384]{1,2,0,3:T(1,128)} %bitcast.922) | data formatting | bytes 262144 | tf_op jit(solution)/shard_map/all_to_all | solution.py:204
  603.4 5.6 all-to-all-start.1
  609.7 12.2 %all-to-all-done.1 = f32[128,2,1,128]{3,2,1,0:T(1,128)S(1)} async-done(((f32[128,2,1,128]{3,2,1,0:T(1,128)}), f32[128,2,1,128]{3,2,1,0:T(1,128)S(1)}, u32[]{:S(2)}, u32[]{:S(2)}) %all-to-all-start.1) | async-done | bytes 131104 | tf_op jit(solution)/shard_map/all_to_all | solution.py:206
  (266 shorter events, 68.4 us)
Async XLA Ops:
  119.3 214.8 %copy-start = (f32[1,128,128]{2,1,0:T(8,128)S(1)}, f32[1,128,128]{2,1,0:T(8,128)}, u32[]{:S(2)}) copy-start(f32[1,128,128]{2,1,0:T(8,128)} %param.14) | copy-start | bytes 196612
  603.4 18.4 %all-to-all-start.1 = ((f32[128,2,1,128]{3,2,1,0:T(1,128)}), f32[128,2,1,128]{3,2,1,0:T(1,128)S(1)}, u32[]{:S(2)}, u32[]{:S(2)}) async-start(f32[128,2,1,128]{3,2,1,0:T(1,128)} %copy.120), calls=%async_computation.1 | async-start | bytes 262144 | tf_op jit(solution)/shard_map/all_to_all | solution.py:206
where the time goes:
time: 630 us; the launch traced here: 623 us
  other arithmetic  368 us (58%)
  local copies, waits for them, and re-layouts  88.7 us (14%)
  blocking collectives  78.6 us (12%)
  matrix products  42 us (7%)
  loops' own time  23.3 us (4%)
  waiting for transfers between devices  12.2 us (2%)
    another operation x31, other arithmetic, invert(): factor = jnp.linalg.cholesky(jnp.concatenate([upper_rows, lower_rows], -2))  171 us
    another operation x17, other arithmetic, invert(): solved = jax.scipy.linalg.cho_solve((factor, True), target)  98.5 us
    unnamed x2, other arithmetic  95.1 us
    all_to_all x1, blocking collectives, on_device(): lax.all_to_all(flattened, 'energy', split_axis=3, concat_axis=0, tiled=True)  40.4 us
    dot_general x95, matrix products, product(): return jnp.matmul(left, right, precision=lax.Precision.HIGHEST)  31.8 us
    all_gather x3, blocking collectives, prefix_2(): gathered = jax.tree.map(lambda a: lax.all_gather(a, axis), part)  29.9 us
    unnamed x11, local copies, waits for them, and re-layouts  27.5 us
    another operation x2, local copies, waits for them, and re-layouts, on_device(): jnp.stack([jnp.stack([value_pair[0] for value_pair in greens], 1), jnp.st...  24 us
  transfers between devices with their start and end apart: 1, of which 1 were waited for; matrix products, arithmetic and copies ran while one was open for 0% of the time, Pallas kernels for 0%

commit v1 on v0

--- a/solution.py
+++ b/solution.py
@@ -201,7 +201,15 @@
     )
     flattened = green.reshape(per_energy, 2, blocks, orders * orders)
     correlated = transform_sum(
-        lax.all_to_all(flattened, "energy", split_axis=3, concat_axis=0, tiled=True)
+        jnp.concatenate(
+            lax.all_to_all(
+                jnp.stack(jnp.split(flattened, lax.axis_size("energy"), axis=3), axis=0),
+                "energy",
+                0,
+                0,
+            ),
+            axis=0,
+        )
     )
     returned = lax.all_to_all(correlated, "energy", split_axis=0, concat_axis=3, tiled=True)
     polar = returned.reshape(per_energy, 2, blocks, orders, orders)

time: 630 us -> 472 us (0.75)
  other arithmetic: 368 us -> 272 us
  local copies, waits for them, and re-layouts: 88.7 us -> 27.8 us
    unnamed x2 -> x0, other arithmetic: 95.1 us -> none
    another operation x6 -> x5, local copies, waits for them, and re-layouts: 24 us -> 0.03 us  [the longest x2 24 us: on_device(): jnp.stack([jnp.stack([value_pair[0] for value_pair in greens], 1), jnp.st...]
    unnamed x11 -> x139, local copies, waits for them, and re-layouts: 27.5 us -> 5.43 us
    all_to_all x1 -> x0, local copies, waits for them, and re-layouts: 15 us -> none  [on_device(): lax.all_to_all(flattened, 'energy', split_axis=3, concat_axis=0, tiled=True)]
where the time goes in v1:
time: 472 us; the launch traced here: 465 us
  other arithmetic  272 us (58%)
  blocking collectives  78.7 us (17%)
  matrix products  41.1 us (9%)
  local copies, waits for them, and re-layouts  27.8 us (6%)
  loops' own time  23 us (5%)
  waiting for transfers between devices  12.2 us (3%)
  starting transfers between devices  5.56 us (1%)
    another operation x31, other arithmetic, invert(): factor = jnp.linalg.cholesky(jnp.concatenate([upper_rows, lower_rows], -2))  171 us
    another operation x17, other arithmetic, invert(): solved = jax.scipy.linalg.cho_solve((factor, True), target)  98.5 us
    all_to_all x1, blocking collectives, on_device(): lax.all_to_all(jnp.stack(jnp.split(flattened, lax.axis_size('energy'), ax...  40.3 us
    dot_general x95, matrix products, product(): return jnp.matmul(left, right, precision=lax.Precision.HIGHEST)  30.9 us
    all_gather x3, blocking collectives, prefix_2(): gathered = jax.tree.map(lambda a: lax.all_gather(a, axis), part)  29.8 us
    another operation x2, loops' own time, prefix_2(): return lax.fori_loop(0, ahead, one, state)  22.6 us
    another operation x36, local copies, waits for them, and re-layouts, invert(): solved = jax.scipy.linalg.cho_solve((factor, True), target)  20.2 us
    all_to_all x1, waiting for transfers between devices, on_device(): lax.all_to_all(correlated, 'energy', split_axis=0, concat_axis=3, tiled=T...  12.2 us
  transfers between devices with their start and end apart: 1, of which 1 were waited for; matrix products, arithmetic and copies ran while one was open for 0% of the time, Pallas kernels for 0%

profile of v1, /device:TPU:1, one launch (start us, length us, event | category | flops | bytes accessed | tf_op | source)
XLA Modules:
  0.0 465.3 jit_solution(10801398621108489814)
XLA Ops:
  0.7 1.0 copy.158
  4.0 11.7 %custom-call.41 = f32[1,128,128]{2,1,0:T(8,128)S(1)} custom-call(f32[1,128,128]{2,1,0:T(8,128)S(1)} %slice.245), custom_call_target="Cholesky" | custom-call | tf_op jit(solution)/shard_map/jit(cholesky)/cholesky/custom-call.2 | solution.py:64
  15.8 9.8 %custom-call.42 = f32[1,1,128,128]{2,3,1,0:T(8,128)S(1)} custom-call(f32[1,1,128,128]{3,2,1,0:T(8,128)S(1)} %get-tuple-element.683), custom_call_target="InvertDiagBlocksLowerTriangular" | custom-call | tf_op jit(solution)/shard_map/jit(cholesky)/cholesky/custom-call.5 | solution.py:64
  26.3 10.5 %all_gather.17 = f32[4,128,128]{2,1,0:T(8,128)S(1)} all-gather(f32[1,128,128]{2,1,0:T(8,128)S(1)} %copy-done), channel_id=1, replica_groups=mesh['energy'=128,'transpor'=4] {'transpor'}, dimensions={0}, use_global_device_ids=true | all-gather | bytes 327680 | tf_op jit(solution)/shard_map/all_gather | solution.py:15
  36.8 1.3 dynamic-slice.18
  38.7 8.6 %all-reduce.1 = f32[4]{0:T(128)S(1)} all-reduce(f32[4]{0:T(128)S(1)} %dynamic-update-slice.23), channel_id=1, replica_groups=mesh['energy'=128,'transpor'=4] {'transpor'}, use_global_device_ids=true, to_apply=%add.1 | all-reduce | flops 4 | bytes 32
  47.3 11.7 %custom-call.43 = f32[1,128,128]{2,1,0:T(8,128)S(1)} custom-call(f32[1,128,128]{2,1,0:T(8,128)S(1)} %fusion.147), custom_call_target="Cholesky" | custom-call | tf_op jit(solution)/shard_map/jit(cholesky)/cholesky/custom-call.3 | solution.py:64
  61.2 3.9 while.67
  61.8 1.3 bitcast_dynamic-update-slice_fusion.16
  63.8 1.3 bitcast_dynamic-update-slice_fusion.16
  65.1 19.7 %custom-call.45 = f32[2,128,128]{1,2,0:T(8,128)S(1)} custom-call(f32[2,128,128]{2,1,0:T(8,128)S(1)} %get-tuple-element.401), custom_call_target="InvertDiagBlocksLowerTriangular" | custom-call | tf_op jit(solution)/shard_map/jit(_cho_solve)/triangular_solve/custom-call.4 | solution.py:66
  86.4 9.4 %all-gather = f32[4,128,128]{2,1,0:T(8,128)S(1)} all-gather(f32[1,128,128]{2,1,0:T(8,128)S(1)} %get-tuple-element.675), channel_id=2, replica_groups=mesh['energy'=128,'transpor'=4] {'transpor'}, dimensions={0}, use_global_device_ids=true | all-gather | bytes 327680 | tf_op jit(solution)/shard_map/all_gather | solution.py:15
  95.7 9.8 %all-gather.1 = f32[4,128,128]{2,1,0:T(8,128)S(1)} all-gather(f32[1,128,128]{2,1,0:T(8,128)S(1)} %get-tuple-element.674), channel_id=3, replica_groups=mesh['energy'=128,'transpor'=4] {'transpor'}, dimensions={0}, use_global_device_ids=true | all-gather | bytes 327680 | tf_op jit(solution)/shard_map/all_gather | solution.py:15
  105.6 12.2 %while.64 = (s32[]{:T(128)}, f32[1,128,128]{2,1,0:T(8,128)S(1)}, f32[1,128,128]{2,1,0:T(8,128)S(1)}, f32[128,128]{1,0:T(8,128)S(1)}, f32[1]{0:T(128)}, /*index=5...) while((s32[]{:T(128)}, f32[1,128,128]{2,1,0:T(8,128)S(1)}, ...), condition=%wide.region_5.9_spmd, body=%wide.region_4.8_spmd.sunk | while | flops 806813952 | bytes 11471332 | solution.py:24
  118.4 214.5 %while.66 = (s32[]{:T(128)}, f32[1,128,128]{2,1,0:T(8,128)S(1)}, f32[1,128,128]{2,1,0:T(8,128)S(1)}, f32[1]{0:T(128)}, s32[]{:T(128)}, /*index=5*/f32[4,1]{0,1:T...) while((s32[]{:T(128)}, f32[1,128,128]{2,1,0:T(8,128)S(1)}, ...), condition=%wide.region_7.11_spmd, body=%wide.region_6.10_spmd.sunk | while | flops 806764800 | bytes 11342354 | solution.py:24
  121.9 11.7 %custom-call.70 = f32[1,128,128]{2,1,0:T(8,128)S(1)} custom-call(f32[1,128,128]{2,1,0:T(8,128)S(1)} %slice.426), custom_call_target="Cholesky" | custom-call | tf_op jit(solution)/shard_map/while/body/jit(cholesky)/cholesky/custom-call.2 | solution.py:64
  133.6 9.8 %custom-call.71 = f32[1,1,128,128]{2,3,1,0:T(8,128)S(1)} custom-call(f32[1,1,128,128]{3,2,1,0:T(8,128)S(1)} %get-tuple-element.948), custom_call_target="InvertDiagBlocksLowerTriangular" | custom-call | tf_op jit(solution)/shard_map/while/body/jit(cholesky)/cholesky/custom-call.5 | solution.py:64
  144.0 11.7 %custom-call.72 = f32[1,128,128]{2,1,0:T(8,128)S(1)} custom-call(f32[1,128,128]{2,1,0:T(8,128)S(1)} %fusion.665), custom_call_target="Cholesky" | custom-call | tf_op jit(solution)/shard_map/while/body/jit(cholesky)/cholesky/custom-call.3 | solution.py:64
  158.0 4.0 while.70
  158.6 1.3 bitcast_dynamic-update-slice_fusion.18
  160.7 1.3 bitcast_dynamic-update-slice_fusion.18
  162.0 19.7 %custom-call.74 = f32[2,128,128]{1,2,0:T(8,128)S(1)} custom-call(f32[2,128,128]{2,1,0:T(8,128)S(1)} %get-tuple-element.954), custom_call_target="InvertDiagBlocksLowerTriangular" | custom-call | tf_op jit(solution)/shard_map/while/body/jit(_cho_solve)/triangular_solve/custom-call.4 | solution.py:66
  187.0 0.9 fusion.678
  193.3 11.7 %custom-call.70 = f32[1,128,128]{2,1,0:T(8,128)S(1)} custom-call(f32[1,128,128]{2,1,0:T(8,128)S(1)} %slice.426), custom_call_target="Cholesky" | custom-call | tf_op jit(solution)/shard_map/while/body/jit(cholesky)/cholesky/custom-call.2 | solution.py:64
  205.1 9.8 %custom-call.71 = f32[1,1,128,128]{2,3,1,0:T(8,128)S(1)} custom-call(f32[1,1,128,128]{3,2,1,0:T(8,128)S(1)} %get-tuple-element.948), custom_call_target="InvertDiagBlocksLowerTriangular" | custom-call | tf_op jit(solution)/shard_map/while/body/jit(cholesky)/cholesky/custom-call.5 | solution.py:64
  215.5 11.7 %custom-call.72 = f32[1,128,128]{2,1,0:T(8,128)S(1)} custom-call(f32[1,128,128]{2,1,0:T(8,128)S(1)} %fusion.665), custom_call_target="Cholesky" | custom-call | tf_op jit(solution)/shard_map/while/body/jit(cholesky)/cholesky/custom-call.3 | solution.py:64
  229.4 4.0 while.70
  230.1 1.3 bitcast_dynamic-update-slice_fusion.18
  232.1 1.3 bitcast_dynamic-update-slice_fusion.18
  233.5 19.7 %custom-call.74 = f32[2,128,128]{1,2,0:T(8,128)S(1)} custom-call(f32[2,128,128]{2,1,0:T(8,128)S(1)} %get-tuple-element.954), custom_call_target="InvertDiagBlocksLowerTriangular" | custom-call | tf_op jit(solution)/shard_map/while/body/jit(_cho_solve)/triangular_solve/custom-call.4 | solution.py:66
  264.8 11.7 %custom-call.70 = f32[1,128,128]{2,1,0:T(8,128)S(1)} custom-call(f32[1,128,128]{2,1,0:T(8,128)S(1)} %slice.426), custom_call_target="Cholesky" | custom-call | tf_op jit(solution)/shard_map/while/body/jit(cholesky)/cholesky/custom-call.2 | solution.py:64
  276.5 9.8 %custom-call.71 = f32[1,1,128,128]{2,3,1,0:T(8,128)S(1)} custom-call(f32[1,1,128,128]{3,2,1,0:T(8,128)S(1)} %get-tuple-element.948), custom_call_target="InvertDiagBlocksLowerTriangular" | custom-call | tf_op jit(solution)/shard_map/while/body/jit(cholesky)/cholesky/custom-call.5 | solution.py:64
  286.9 11.7 %custom-call.72 = f32[1,128,128]{2,1,0:T(8,128)S(1)} custom-call(f32[1,128,128]{2,1,0:T(8,128)S(1)} %fusion.665), custom_call_target="Cholesky" | custom-call | tf_op jit(solution)/shard_map/while/body/jit(cholesky)/cholesky/custom-call.3 | solution.py:64
  300.9 4.0 while.70
  301.5 1.3 bitcast_dynamic-update-slice_fusion.18
  303.6 1.3 bitcast_dynamic-update-slice_fusion.18
  304.9 19.7 %custom-call.74 = f32[2,128,128]{1,2,0:T(8,128)S(1)} custom-call(f32[2,128,128]{2,1,0:T(8,128)S(1)} %get-tuple-element.954), custom_call_target="InvertDiagBlocksLowerTriangular" | custom-call | tf_op jit(solution)/shard_map/while/body/jit(_cho_solve)/triangular_solve/custom-call.4 | solution.py:66
  330.0 0.9 fusion.678
  335.8 11.7 %custom-call.46 = f32[1,128,128]{2,1,0:T(8,128)S(1)} custom-call(f32[1,128,128]{2,1,0:T(8,128)S(1)} %slice.255), custom_call_target="Cholesky" | custom-call | tf_op jit(solution)/shard_map/jit(cholesky)/cholesky/custom-call.2 | solution.py:64
  347.6 9.8 %custom-call.47 = f32[1,1,128,128]{2,3,1,0:T(8,128)S(1)} custom-call(f32[1,1,128,128]{3,2,1,0:T(8,128)S(1)} %get-tuple-element.679), custom_call_target="InvertDiagBlocksLowerTriangular" | custom-call | tf_op jit(solution)/shard_map/jit(cholesky)/cholesky/custom-call.5 | solution.py:64
  358.1 11.7 %custom-call.48 = f32[1,128,128]{2,1,0:T(8,128)S(1)} custom-call(f32[1,128,128]{2,1,0:T(8,128)S(1)} %fusion.150), custom_call_target="Cholesky" | custom-call | tf_op jit(solution)/shard_map/jit(cholesky)/cholesky/custom-call.3 | solution.py:64
  372.6 4.3 while.68
  373.4 1.4 bitcast_dynamic-update-slice_fusion.17
  375.5 1.4 bitcast_dynamic-update-slice_fusion.17
  376.9 19.7 %custom-call.50 = f32[2,128,128]{1,2,0:T(8,128)S(1)} custom-call(f32[2,128,128]{2,1,0:T(8,128)S(1)} %get-tuple-element.403), custom_call_target="InvertDiagBlocksLowerTriangular" | custom-call | tf_op jit(solution)/shard_map/jit(_cho_solve)/triangular_solve/custom-call.4 | solution.py:66
  400.0 40.3 %all_to_all.20 = f32[128,1,2,1,128]{4,2,3,1,0:T(2,128)S(1)} all-to-all(f32[128,1,2,1,128]{4,2,3,1,0:T(2,128)S(1)} %constant_dynamic-update-slice_fusion.2), channel_id=1, replica_groups=mesh['energy'=128,'transpor'=4] {'energy'}, dimensions={0} | all-to-all | bytes 262144 | tf_op jit(solution)/shard_map/all_to_all | solution.py:205
  446.1 5.6 %all-to-all-start.1 = ((f32[128,2,1,128]{3,2,1,0:T(1,128)}), f32[128,2,1,128]{3,2,1,0:T(1,128)S(1)}, u32[]{:S(2)}, u32[]{:S(2)}) async-start(f32[128,2,1,128]{3,2,1,0:T(1,128)} %copy.299), calls=%async_computation.1 | async-start | bytes 262144 | tf_op jit(solution)/shard_map/all_to_all | solution.py:214
  452.3 12.2 %all-to-all-done.1 = f32[128,2,1,128]{3,2,1,0:T(1,128)S(1)} async-done(((f32[128,2,1,128]{3,2,1,0:T(1,128)}), f32[128,2,1,128]{3,2,1,0:T(1,128)S(1)}, u32[]{:S(2)}, u32[]{:S(2)}) %all-to-all-start.1) | async-done | bytes 131104 | tf_op jit(solution)/shard_map/all_to_all | solution.py:214
  (406 shorter events, 59.2 us)
Async XLA Ops:
  0.6 1.0 copy-start.1
  1.8 0.8 copy-start
  2.0 0.7 copy-start.2
  446.1 18.4 %all-to-all-start.1 = ((f32[128,2,1,128]{3,2,1,0:T(1,128)}), f32[128,2,1,128]{3,2,1,0:T(1,128)S(1)}, u32[]{:S(2)}, u32[]{:S(2)}) async-start(f32[128,2,1,128]{3,2,1,0:T(1,128)} %copy.299), calls=%async_computation.1 | async-start | bytes 262144 | tf_op jit(solution)/shard_map/all_to_all | solution.py:214
